TPU v7x, 128 devices: a whole 4x4x4 slice. The times are simulated.
128 devices in a mesh: dp: 8 (over z_lo, x), expert: 16 (over z_hi, y, core).
Axes of the slice: x: 4, y: 4, z: 4 (z_hi: 2, z_lo: 2; z = z_hi * 2 + z_lo), core: 2. Of those that a mesh axis runs over, the one named last changes fastest.
Arguments:
- tokens: bfloat16 [16384, 2048], P(('dp', 'expert')), may hold values from -6 to 6
- cotangent: bfloat16 [16384, 2048], P(('dp', 'expert')), may hold values from -6 to 6
- expert_ids: int32 [16384, 4], P(('dp', 'expert')), may hold values from 0 to 15, all different within a row; in each aligned block of 128 rows (0 to 127, 128 to 255, ...) at most 48 rows name the same one
- gate_probs: bfloat16 [16384, 4], P(('dp', 'expert')), may hold values from 0.049804688 to 0.5
- w_in: bfloat16 [16, 2048, 1536], P('expert', 'dp'), may hold values from -0.125 to 0.125
- w_out: bfloat16 [16, 768, 2048], P('expert', 'dp'), may hold values from -0.21875 to 0.21875
- mom_in: float32 [16, 2048, 1536], P('expert', 'dp'), may hold values from -12 to 12
- mom_out: float32 [16, 768, 2048], P('expert', 'dp'), may hold values from -12 to 12
Outputs:
- layer_out: bfloat16 [16384, 2048], P(('dp', 'expert'))
- tokens_grad: bfloat16 [16384, 2048], P(('dp', 'expert'))
- gate_grad: bfloat16 [16384, 4], P(('dp', 'expert'))
- w_in_new: bfloat16 [16, 2048, 1536], P('expert', 'dp')
- w_out_new: bfloat16 [16, 768, 2048], P('expert', 'dp')
- mom_in_new: float32 [16, 2048, 1536], P('expert', 'dp')
- mom_out_new: float32 [16, 768, 2048], P('expert', 'dp')
Inputs may be any that keep to these rules, and one draw needn't show every extreme that they name: `expert_ids`: each row names 4 different experts. Among the 128 tokens of one device (aligned blocks of rows), no expert is named more than 48 times, a bound that some block reaches.
All inputs are finite; a program needn't handle non-finite values.
Results may differ from a plain program's by a relative error of at most 0.009.
Values may be sent and summed in bfloat16 or wider, within the bound.
No kernel may reach another device: no remote copies, remote signals or barrier semaphores. Data moves between devices by JAX's collectives and lax.ppermute only.
A program may use at most 128 MiB of HBM per device.

v0:
```python
import jax
import jax.numpy as jnp
from jax import lax
from jax.sharding import PartitionSpec as P

FF = 768


beta_one = 0.9
beta_two = 0.99
learn_rate = 0.02
decay_rate = 0.1


def to_experts(buffer, groups, local_count, capacity):
    trailing = buffer.shape[2:]
    shaped = buffer.reshape((groups, local_count, capacity) + trailing)
    return jnp.swapaxes(shaped, 0, 1).reshape((local_count, groups * capacity) + trailing)


def from_experts(buffer, groups, local_count, capacity):
    trailing = buffer.shape[2:]
    shaped = buffer.reshape((local_count, groups, capacity) + trailing)
    return jnp.swapaxes(shaped, 0, 1).reshape((groups, local_count * capacity) + trailing)


def forward_pass(expert_in, expert_gates, full_in, full_out):
    pre = jnp.einsum("erd,edf->erf", expert_in, full_in, preferred_element_type=jnp.float32)
    gate_part = pre[..., :FF]
    up_part = pre[..., FF:]
    sig_part = jax.nn.sigmoid(gate_part)
    activated = gate_part * sig_part
    hidden = (activated * up_part).astype(jnp.bfloat16)
    expert_out = jnp.einsum("erf,efd->erd", hidden, full_out, preferred_element_type=jnp.float32)
    gate_col = expert_gates.astype(jnp.float32)[..., None]
    weighted = (gate_col * expert_out).astype(jnp.bfloat16)
    return (up_part, gate_part, sig_part, activated, hidden, expert_out, weighted)


def lion_update(weight, moment, grad):
    blend = beta_one * moment + (1.0 - beta_one) * grad
    direction = blend / jnp.sqrt(blend * blend + 1.0)
    wide = weight.astype(jnp.float32)
    new_weight = (wide - learn_rate * (direction + decay_rate * wide)).astype(jnp.bfloat16)
    new_moment = beta_two * moment + (1.0 - beta_two) * grad
    return (new_weight, new_moment)


def body(tokens, cotangent, expert_ids, gate_probs, w_in, w_out, mom_in, mom_out):
    groups = lax.axis_size("expert")
    local_count = w_in.shape[0]
    experts = groups * local_count
    tok_rows, top_count = expert_ids.shape
    model_width = tokens.shape[1]
    capacity = 3 * tok_rows * top_count // (2 * experts)
    slot_total = experts * capacity
    flat_ids = expert_ids.reshape(-1)
    onehot = (flat_ids[:, None] == jnp.arange(experts, dtype=jnp.int32)[None, :]).astype(jnp.int32)
    position = jnp.sum((jnp.cumsum(onehot, axis=0) - onehot) * onehot, axis=1)
    slot_ids = flat_ids * capacity + position
    matches = (slot_ids[:, None] == jnp.arange(slot_total, dtype=jnp.int32)[None, :]).reshape(
        tok_rows, top_count, slot_total
    )
    placement = jnp.sum(matches.astype(jnp.int32), axis=1).astype(jnp.bfloat16)
    match_float = matches.astype(jnp.float32)
    gate_slots = jnp.einsum("tk,tks->s", gate_probs.astype(jnp.float32), match_float).astype(
        jnp.bfloat16
    )
    gate_slots = gate_slots.reshape(groups, local_count * capacity)
    x_slots = jnp.einsum("ts,td->sd", placement, tokens, preferred_element_type=jnp.float32).astype(
        jnp.bfloat16
    )
    x_slots = x_slots.reshape(groups, local_count * capacity, model_width)
    cot_slots = jnp.einsum(
        "ts,td->sd", placement, cotangent, preferred_element_type=jnp.float32
    ).astype(jnp.bfloat16)
    cot_slots = cot_slots.reshape(groups, local_count * capacity, model_width)
    full_in, full_out = (
        lax.all_gather(w_in, "dp", axis=1, tiled=True),
        lax.all_gather(w_out, "dp", axis=1, tiled=True),
    )
    recv_x, recv_gate, recv_cot = (
        lax.all_to_all(x_slots, "expert", split_axis=0, concat_axis=0, tiled=True),
        lax.all_to_all(gate_slots, "expert", split_axis=0, concat_axis=0, tiled=True),
        lax.all_to_all(cot_slots, "expert", split_axis=0, concat_axis=0, tiled=True),
    )
    expert_in = to_experts(recv_x, groups, local_count, capacity)
    expert_gates = to_experts(recv_gate, groups, local_count, capacity)
    up_part, gate_part, sig_part, activated, hidden, expert_out, weighted = forward_pass(
        expert_in, expert_gates, full_in, full_out
    )
    expert_cot = to_experts(recv_cot, groups, local_count, capacity)
    slot_gate = jnp.sum(expert_cot.astype(jnp.float32) * expert_out, axis=-1).astype(jnp.bfloat16)
    out_grad = (
        expert_gates.astype(jnp.float32)[..., None] * expert_cot.astype(jnp.float32)
    ).astype(jnp.bfloat16)
    hidden_grad = jnp.einsum("erd,efd->erf", out_grad, full_out, preferred_element_type=jnp.float32)
    slope = sig_part * (1.0 + gate_part * (1.0 - sig_part))
    pre_grad = jnp.concatenate(
        [hidden_grad * up_part * slope, hidden_grad * activated], axis=-1
    ).astype(jnp.bfloat16)
    slot_grad = jnp.einsum(
        "erf,edf->erd", pre_grad, full_in, preferred_element_type=jnp.float32
    ).astype(jnp.bfloat16)
    returned = (
        lax.all_to_all(
            from_experts(weighted, groups, local_count, capacity),
            "expert",
            split_axis=0,
            concat_axis=0,
            tiled=True,
        ),
        lax.all_to_all(
            from_experts(slot_grad, groups, local_count, capacity),
            "expert",
            split_axis=0,
            concat_axis=0,
            tiled=True,
        ),
        lax.all_to_all(
            from_experts(slot_gate, groups, local_count, capacity),
            "expert",
            split_axis=0,
            concat_axis=0,
            tiled=True,
        ),
    )
    layer_slots = returned[0].reshape(slot_total, model_width)
    grad_slots = returned[1].reshape(slot_total, model_width)
    gate_back = returned[2].reshape(slot_total).astype(jnp.float32)
    layer_out = jnp.einsum(
        "ts,sd->td", placement, layer_slots, preferred_element_type=jnp.float32
    ).astype(jnp.bfloat16)
    tokens_grad = jnp.einsum(
        "ts,sd->td", placement, grad_slots, preferred_element_type=jnp.float32
    ).astype(jnp.bfloat16)
    gate_grad = jnp.einsum("tks,s->tk", match_float, gate_back).astype(jnp.bfloat16)
    term_in = jnp.einsum("erd,erf->edf", expert_in, pre_grad, preferred_element_type=jnp.float32)
    term_out = jnp.einsum("erf,erd->efd", hidden, out_grad, preferred_element_type=jnp.float32)
    grad_in, grad_out = (
        lax.psum_scatter(
            term_in.astype(jnp.bfloat16), "dp", scatter_dimension=1, tiled=True
        ).astype(jnp.float32),
        lax.psum_scatter(
            term_out.astype(jnp.bfloat16), "dp", scatter_dimension=1, tiled=True
        ).astype(jnp.float32),
    )
    w_in_new, mom_in_new = lion_update(w_in, mom_in, grad_in)
    w_out_new, mom_out_new = lion_update(w_out, mom_out, grad_out)
    return (layer_out, tokens_grad, gate_grad, w_in_new, w_out_new, mom_in_new, mom_out_new)


def solution(mesh):
    in_specs = (
        P(("dp", "expert"), None),
        P(("dp", "expert"), None),
        P(("dp", "expert"), None),
        P(("dp", "expert"), None),
        P("expert", "dp", None),
        P("expert", "dp", None),
        P("expert", "dp", None),
        P("expert", "dp", None),
    )
    out_specs = (
        P(("dp", "expert"), None),
        P(("dp", "expert"), None),
        P(("dp", "expert"), None),
        P("expert", "dp", None),
        P("expert", "dp", None),
        P("expert", "dp", None),
        P("expert", "dp", None),
    )
    return jax.shard_map(body, mesh=mesh, in_specs=in_specs, out_specs=out_specs, check_vma=False)
```

profile of v0, /device:TPU:9, one launch (start us, length us, event | category | flops | bytes accessed | tf_op | source)
XLA Modules:
  0.0 401.0 jit_solution(7252616509679927067)
XLA Ops:
  7.2 0.7 all-gather.3.cloned.1.call-update
  7.9 0.8 copy.44
  8.9 1.2 reduce-window.6
  10.6 0.7 multiply_add_fusion
  11.3 1.1 fusion.34
  12.4 0.7 all_to_all.29
  13.1 8.6 %all-to-all-start = ((bf16[16,1,48]{2,1,0:T(2,128)(2,1)}), bf16[16,1,48]{2,1,0:T(2,128)(2,1)S(1)}, u32[]{:S(2)}, u32[]{:S(2)}) async-start(bf16[16,1,48]{2,1,0:T(2,128)(2,1)} %all_to_all.29), calls=%async_computation | async-start | bytes 16384 | tf_op jit(solution)/shard_map/all_to_all | solution.py:84
  22.0 2.7 convolution_convert_fusion.3
  24.7 2.9 all-to-all-done
  27.6 6.1 %all-to-all-start.1 = ((bf16[16,48,2048]{2,1,0:T(8,128)(2,1)}), bf16[16,48,2048]{2,1,0:T(8,128)(2,1)}, u32[]{:S(2)}, u32[]{:S(2)}) async-start(bf16[16,48,2048]{2,1,0:T(8,128)(2,1)} %bitcast.102), calls=%async_computation.1 | async-start | bytes 6291456 | tf_op jit(solution)/shard_map/all_to_all | solution.py:83
  33.7 0.7 all-gather.5.cloned.1.call-update
  34.5 2.8 convolution_convert_fusion.2
  37.2 82.1 %all-to-all-done.1 = bf16[16,48,2048]{2,1,0:T(8,128)(2,1)} async-done(((bf16[16,48,2048]{2,1,0:T(8,128)(2,1)}), bf16[16,48,2048]{2,1,0:T(8,128)(2,1)}, u32[]{:S(2)}, u32[]{:S(2)}) %all-to-all-start.1) | async-done | bytes 3145760 | tf_op jit(solution)/shard_map/all_to_all | solution.py:83
  119.4 4.8 %all-to-all-start.3 = ((bf16[16,48,2048]{2,1,0:T(8,128)(2,1)}), bf16[16,48,2048]{2,1,0:T(8,128)(2,1)}, u32[]{:S(2)}, u32[]{:S(2)}) async-start(bf16[16,48,2048]{2,1,0:T(8,128)(2,1)} %bitcast.101), calls=%async_computation.3 | async-start | bytes 6291456 | tf_op jit(solution)/shard_map/all_to_all | solution.py:85
  124.4 9.7 %fusion.6 = f32[1,768,1536]{2,1,0:T(8,128)} fusion(bf16[768,2048]{1,0:T(8,128)(2,1)} %bitcast.3, bf16[1,2048,1536]{2,1,0:T(8,128)(2,1)} %all-gather.3.cloned.1.call-done), kind=kOutput, calls=%fused_computation.10 | convolution fusion | flops 4831838208 | bytes 14155776 | tf_op jit(solution)/shard_map/erd,edf->erf/dot_general | solution.py:28
  134.0 53.7 %all-to-all-done.3 = bf16[16,48,2048]{2,1,0:T(8,128)(2,1)} async-done(((bf16[16,48,2048]{2,1,0:T(8,128)(2,1)}), bf16[16,48,2048]{2,1,0:T(8,128)(2,1)}, u32[]{:S(2)}, u32[]{:S(2)}) %all-to-all-start.3) | async-done | bytes 3145760 | tf_op jit(solution)/shard_map/all_to_all | solution.py:85
  187.8 8.9 %fusion.33 = (bf16[768,768]{1,0:T(8,128)(2,1)}, bf16[768,768]{1,0:T(8,128)(2,1)}, bf16[768,768]{1,0:T(8,128)(2,1)S(1)}) fusion(f32[1,768,1536]{2,1,0:T(8,128)} %fusion.6, bf16[1,768,2048]{2,1,0:T(8,128)(2,1)} %all-gather.5.cloned.1.call-done, f32[768]{0:T(1024)S(1)} %reshape.241, bf16[1,768,1,1,1,1,2048]{6,1,5,4,3,2,0:T(8,128)(2,1)} %bitcast.80), kind=kOutput, calls=%fused_computation.49 | convolution fusion | flops 2429485056 | bytes 14552064 | tf_op jit(solution)/shard_map/erd,efd->erf/dot_general | solution.py:97
  196.7 6.1 %fusion.17 = bf16[1,768,2048]{2,1,0:T(8,128)(2,1)} fusion(bf16[768,768]{1,0:T(8,128)(2,1)S(1)} %get-tuple-element.11, f32[768]{0:T(1024)S(1)} %reshape.241, bf16[1,768,1,1,1,1,2048]{6,1,5,4,3,2,0:T(8,128)(2,1)} %bitcast.80), kind=kOutput, calls=%fused_computation.20 | convolution fusion | flops 2422210560 | bytes 7474176 | tf_op jit(solution)/shard_map/erf,erd->efd/dot_general | solution.py:139
  203.0 9.1 %fusion = bf16[1,2048,1536]{2,1,0:T(8,128)(2,1)} fusion(bf16[768,2048]{1,0:T(8,128)(2,1)} %bitcast.3, bf16[768,768]{1,0:T(8,128)(2,1)} %get-tuple-element.8, bf16[768,768]{1,0:T(8,128)(2,1)} %get-tuple-element.7), kind=kOutput, calls=%fused_computation.1 | convolution fusion | flops 4839702528 | bytes 11796480 | tf_op jit(solution)/shard_map/erd,erf->edf/dot_general | solution.py:138
  212.1 6.7 %fusion.1 = (bf16[768]{0:T(1024)(128)(2,1)S(1)}, bf16[768,2048]{1,0:T(8,128)(2,1)}) fusion(bf16[16,48,2048]{2,1,0:T(8,128)(2,1)} %all-to-all-done.3, f32[768]{0:T(1024)S(1)} %reshape.241, bf16[768,768]{1,0:T(8,128)(2,1)S(1)} %get-tuple-element.11, bf16[1,768,2048]{2,1,0:T(8,128)(2,1)} %all-gather.5.cloned.1.call-done), kind=kOutput, calls=%fused_computation.3 | convolution fusion | flops 2423782656 | bytes 10621440 | tf_op jit(solution)/shard_map/erf,efd->erd/dot_general | solution.py:34
  219.0 10.6 %all_to_all.36 = bf16[16,1,48]{2,1,0:T(2,128)(2,1)S(1)} all-to-all(bf16[16,1,48]{2,1,0:T(2,128)(2,1)S(1)} %convert_element_type.204), channel_id=1, replica_groups=mesh['dp'=8,'expert'=16] {'expert'}, dimensions={0} | all-to-all | bytes 3072 | tf_op jit(solution)/shard_map/all_to_all | solution.py:120
  229.6 6.1 %all-to-all-start.2 = ((bf16[16,48,2048]{2,1,0:T(8,128)(2,1)}), bf16[16,48,2048]{2,1,0:T(8,128)(2,1)}, u32[]{:S(2)}, u32[]{:S(2)}) async-start(bf16[16,48,2048]{2,1,0:T(8,128)(2,1)} %bitcast.104), calls=%async_computation.2 | async-start | bytes 6291456 | tf_op jit(solution)/shard_map/all_to_all | solution.py:106
  235.7 8.8 %fusion.9 = bf16[768,2048]{1,0:T(8,128)(2,1)} fusion(bf16[1,2048,1536]{2,1,0:T(8,128)(2,1)} %all-gather.3.cloned.1.call-done, bf16[768,768]{1,0:T(8,128)(2,1)} %get-tuple-element.8, bf16[768,768]{1,0:T(8,128)(2,1)S(1)} %copy-done.5), kind=kOutput, calls=%fused_computation.14 | convolution fusion | flops 4838129664 | bytes 11796480 | tf_op jit(solution)/shard_map/erf,edf->erd/dot_general | solution.py:102
  244.5 92.9 %all-to-all-done.2 = bf16[16,48,2048]{2,1,0:T(8,128)(2,1)} async-done(((bf16[16,48,2048]{2,1,0:T(8,128)(2,1)}), bf16[16,48,2048]{2,1,0:T(8,128)(2,1)}, u32[]{:S(2)}, u32[]{:S(2)}) %all-to-all-start.2) | async-done | bytes 3145760 | tf_op jit(solution)/shard_map/all_to_all | solution.py:106
  337.4 4.9 %all-to-all-start.4 = ((bf16[16,48,2048]{2,1,0:T(8,128)(2,1)}), bf16[16,48,2048]{2,1,0:T(8,128)(2,1)}, u32[]{:S(2)}, u32[]{:S(2)}) async-start(bf16[16,48,2048]{2,1,0:T(8,128)(2,1)} %bitcast.103), calls=%async_computation.4 | async-start | bytes 6291456 | tf_op jit(solution)/shard_map/all_to_all | solution.py:113
  342.4 0.4 fusion.29
  342.8 0.6 convert_element_type.190
  343.4 3.3 convolution_convert_fusion.5
  346.7 38.3 %all-to-all-done.4 = bf16[16,48,2048]{2,1,0:T(8,128)(2,1)} async-done(((bf16[16,48,2048]{2,1,0:T(8,128)(2,1)}), bf16[16,48,2048]{2,1,0:T(8,128)(2,1)}, u32[]{:S(2)}, u32[]{:S(2)}) %all-to-all-start.4) | async-done | bytes 3145760 | tf_op jit(solution)/shard_map/all_to_all | solution.py:113
  384.9 3.4 convolution_convert_fusion.4
  388.4 2.7 fusion.39
  391.1 3.4 fusion.26
  (38 shorter events, 1.7 us)
Async XLA Ops:
  7.2 14.8 %copy-start = (bf16[128,2048]{1,0:T(8,128)(2,1)S(1)}, bf16[128,2048]{1,0:T(8,128)(2,1)}, u32[]{:S(2)}) copy-start(bf16[128,2048]{1,0:T(8,128)(2,1)} %param.8) | copy-start | bytes 1572868
  7.2 117.2 %all-gather.3.cloned.1.call-start = ((), (), s32[]{:S(2)}) async-start(), calls=%async_computation.8 | async-start | bytes 7077888 | tf_op jit(solution)/shard_map/all_gather | solution.py:79
  13.1 14.4 %all-to-all-start = ((bf16[16,1,48]{2,1,0:T(2,128)(2,1)}), bf16[16,1,48]{2,1,0:T(2,128)(2,1)S(1)}, u32[]{:S(2)}, u32[]{:S(2)}) async-start(bf16[16,1,48]{2,1,0:T(2,128)(2,1)} %all_to_all.29), calls=%async_computation | async-start | bytes 16384 | tf_op jit(solution)/shard_map/all_to_all | solution.py:84
  27.6 6.9 %copy-start.4 = (bf16[128,2048]{1,0:T(8,128)(2,1)S(1)}, bf16[128,2048]{1,0:T(8,128)(2,1)}, u32[]{:S(2)}) copy-start(bf16[128,2048]{1,0:T(8,128)(2,1)} %param.9) | copy-start | bytes 1572868
  27.6 91.8 %all-to-all-start.1 = ((bf16[16,48,2048]{2,1,0:T(8,128)(2,1)}), bf16[16,48,2048]{2,1,0:T(8,128)(2,1)}, u32[]{:S(2)}, u32[]{:S(2)}) async-start(bf16[16,48,2048]{2,1,0:T(8,128)(2,1)} %bitcast.102), calls=%async_computation.1 | async-start | bytes 6291456 | tf_op jit(solution)/shard_map/all_to_all | solution.py:83
  33.7 154.1 %all-gather.5.cloned.1.call-start = ((), (), s32[]{:S(2)}) async-start(), calls=%async_computation.9 | async-start | bytes 3538944 | tf_op jit(solution)/shard_map/all_gather | solution.py:80
  119.4 68.4 %all-to-all-start.3 = ((bf16[16,48,2048]{2,1,0:T(8,128)(2,1)}), bf16[16,48,2048]{2,1,0:T(8,128)(2,1)}, u32[]{:S(2)}, u32[]{:S(2)}) async-start(bf16[16,48,2048]{2,1,0:T(8,128)(2,1)} %bitcast.101), calls=%async_computation.3 | async-start | bytes 6291456 | tf_op jit(solution)/shard_map/all_to_all | solution.py:85
  124.2 264.2 %reduce-scatter.5.cloned.1.call-start = ((), (), s32[]{:S(2)}) async-start(), calls=%async_computation.11 | async-start | bytes 3538944 | tf_op jit(solution)/shard_map/reduce_scatter | solution.py:144
  202.8 188.2 %reduce-scatter.3.cloned.1.call-start = ((), (), s32[]{:S(2)}) async-start(), calls=%async_computation.10 | async-start | bytes 7077888 | tf_op jit(solution)/shard_map/reduce_scatter | solution.py:141
  229.6 6.1 %copy-start.5 = (bf16[768,768]{1,0:T(8,128)(2,1)S(1)}, bf16[768,768]{1,0:T(8,128)(2,1)}, u32[]{:S(2)}) copy-start(bf16[768,768]{1,0:T(8,128)(2,1)} %get-tuple-element.7) | copy-start | bytes 3538948
  229.6 107.8 %all-to-all-start.2 = ((bf16[16,48,2048]{2,1,0:T(8,128)(2,1)}), bf16[16,48,2048]{2,1,0:T(8,128)(2,1)}, u32[]{:S(2)}, u32[]{:S(2)}) async-start(bf16[16,48,2048]{2,1,0:T(8,128)(2,1)} %bitcast.104), calls=%async_computation.2 | async-start | bytes 6291456 | tf_op jit(solution)/shard_map/all_to_all | solution.py:106
  337.4 47.6 %all-to-all-start.4 = ((bf16[16,48,2048]{2,1,0:T(8,128)(2,1)}), bf16[16,48,2048]{2,1,0:T(8,128)(2,1)}, u32[]{:S(2)}, u32[]{:S(2)}) async-start(bf16[16,48,2048]{2,1,0:T(8,128)(2,1)} %bitcast.103), calls=%async_computation.4 | async-start | bytes 6291456 | tf_op jit(solution)/shard_map/all_to_all | solution.py:113
  346.7 41.7 %copy-start.3 = (bf16[1,96,2048]{2,1,0:T(8,128)(2,1)S(1)}, bf16[1,96,2048]{2,1,0:T(8,128)(2,1)}, u32[]{:S(2)}) copy-start(bf16[1,96,2048]{2,1,0:T(8,128)(2,1)} %param.13) | copy-start | bytes 1179652
  384.9 6.1 %copy-start.1 = (bf16[1,256,1536]{2,1,0:T(8,128)(2,1)S(1)}, bf16[1,256,1536]{2,1,0:T(8,128)(2,1)}, u32[]{:S(2)}) copy-start(bf16[1,256,1536]{2,1,0:T(8,128)(2,1)} %param.12) | copy-start | bytes 2359300
  384.9 6.1 %copy-start.2 = (f32[1,256,1536]{2,1,0:T(8,128)S(1)}, f32[1,256,1536]{2,1,0:T(8,128)}, u32[]{:S(2)}) copy-start(f32[1,256,1536]{2,1,0:T(8,128)} %param.14) | copy-start | bytes 4718596
Sparse Core Ops, SparseCore 0:
  9.7 99.9 all-gather.2
  111.3 65.3 all-gather.4
  202.9 40.7 reduce-scatter.4
  246.0 87.7 reduce-scatter.2
where the time goes:
time: 402 us; the launch traced here: 401 us
  waiting for transfers between devices  271 us (67%)
  matrix products  62.9 us (16%)
  starting transfers between devices  30.9 us (8%)
  between operations  13.9 us (3%)
  blocking collectives  10.6 us (3%)
  other arithmetic  8.94 us (2%)
    all_to_all x1, waiting for transfers between devices, body(): lax.all_to_all(from_experts(weighted, groups, local_count, capacity), 'ex...  92.9 us
    all_to_all x1, waiting for transfers between devices, body(): lax.all_to_all(x_slots, 'expert', split_axis=0, concat_axis=0, tiled=True)  82.1 us
    all_to_all x1, waiting for transfers between devices, body(): lax.all_to_all(cot_slots, 'expert', split_axis=0, concat_axis=0, tiled=True)  53.7 us
    all_to_all x1, waiting for transfers between devices, body(): lax.all_to_all(from_experts(slot_grad, groups, local_count, capacity), 'e...  38.3 us
    all_to_all x1, blocking collectives, body(): lax.all_to_all(from_experts(slot_gate, groups, local_count, capacity), 'e...  10.6 us
    dot_general x1, matrix products, forward_pass(): jnp.einsum('erd,edf->erf', expert_in, full_in, preferred_element_type=jnp...  9.66 us
    dot_general x1, matrix products, body(): jnp.einsum('erd,erf->edf', expert_in, pre_grad, preferred_element_type=jn...  9.08 us
    dot_general x1, matrix products, body(): jnp.einsum('erd,efd->erf', out_grad, full_out, preferred_element_type=jnp...  8.92 us
  transfers between devices with their start and end apart: 9, of which 5 were waited for; matrix products, arithmetic and copies ran while one was open for 14% of the time, Pallas kernels for 0%

commit v1 on v0

v1 whole, which is shorter than its diff:
```python
import jax
import jax.numpy as jnp
from jax import lax
from jax.sharding import PartitionSpec as P

beta_one = 0.9
beta_two = 0.99
learn_rate = 0.02
decay_rate = 0.1

NZ, NY, NC = 2, 4, 2
F32 = jnp.float32
BF16 = jnp.bfloat16


def hop(value, dz=0, dy=0, dc=0):
    pairs = []
    for i in range(NZ * NY * NC):
        z, y, c = i // (NY * NC), (i // NC) % NY, i % NC
        to = ((z + dz) % NZ) * NY * NC + ((y + dy) % NY) * NC + (c + dc) % NC
        pairs.append((i, to))
    return lax.ppermute(value, "expert", pairs)


def lion_update(weight, moment, grad):
    blend = beta_one * moment + (1.0 - beta_one) * grad
    direction = blend / jnp.sqrt(blend * blend + 1.0)
    wide = weight.astype(F32)
    new_weight = (wide - learn_rate * (direction + decay_rate * wide)).astype(BF16)
    new_moment = beta_two * moment + (1.0 - beta_two) * grad
    return (new_weight, new_moment)


def dot(a, b, dims):
    return lax.dot_general(a, b, (dims, ((), ())), preferred_element_type=F32)


def gather_blocks(own):
    near = jnp.concatenate([own, hop(own, dz=1)], axis=0)
    return jnp.concatenate([near, hop(near, dc=1)], axis=0)


def scatter_blocks(part):
    half = part.shape[0] // 2
    near = part[:half] + hop(part[half:].astype(BF16), dc=1).astype(F32)
    rows = half // 2
    return near[:rows] + hop(near[rows:].astype(BF16), dz=1).astype(F32)


def body(tokens, cotangent, expert_ids, gate_probs, w_in, w_out, mom_in, mom_out):
    tok_rows, top_count = expert_ids.shape
    experts = NZ * NY * NC
    cap = 3 * tok_rows * top_count // (2 * experts)
    blocks = NZ * NC
    width = blocks * tok_rows
    ff = w_in.shape[2] // 2
    me = lax.axis_index("expert")
    z, y, c = me // (NY * NC), (me // NC) % NY, me % NC

    full_in = lax.all_gather(w_in, "dp", axis=1, tiled=True)[0]
    full_out = lax.all_gather(w_out, "dp", axis=1, tiled=True)[0]

    meta = jnp.concatenate([expert_ids.T.astype(BF16), gate_probs.T], axis=0)
    meta = gather_blocks(meta[None])
    x_all = gather_blocks(tokens)
    cot_all = gather_blocks(cotangent)
    ids = meta[:, :top_count].astype(jnp.int32)
    gates = meta[:, top_count:].astype(F32)
    steps = jnp.arange(NY, dtype=jnp.int32)
    wanted = z * (NY * NC) + ((y + steps) % NY) * NC + c
    hits = ids[None] == wanted[:, None, None, None]
    member = jnp.any(hits, axis=2)
    gate_of = jnp.sum(jnp.where(hits, gates[None], 0.0), axis=2)
    before = (jnp.arange(tok_rows)[:, None] < jnp.arange(tok_rows)[None, :]).astype(BF16)
    position = dot(
        member.reshape(NY * blocks, tok_rows).astype(BF16), before, ((1,), (0,))
    ).astype(jnp.int32)
    position = jnp.where(member.reshape(NY * blocks, tok_rows), position, -1)
    position = position.reshape(NY, blocks, tok_rows)
    same = jnp.eye(blocks, dtype=bool)
    spread = jnp.where(same[None, :, :, None], position[:, None], -1)
    spread = spread.reshape(NY * blocks, width)
    place = spread[:, None, :] == jnp.arange(cap, dtype=jnp.int32)[None, :, None]
    slots = NY * blocks * cap
    gate_wide = jnp.broadcast_to(
        gate_of.reshape(NY, 1, 1, width), (NY, blocks, cap, width)
    ).reshape(slots, width)
    place = place.reshape(slots, width)
    pick = place.astype(BF16)
    pick_gate = jnp.where(place, gate_wide, 0.0).astype(BF16)

    chunk = blocks * cap

    def to_experts(rows):
        parts = [rows[:chunk]]
        for step in range(1, NY):
            parts.append(hop(rows[step * chunk : (step + 1) * chunk], dy=step))
        return jnp.concatenate(parts, axis=0)

    def from_experts(rows):
        parts = [rows[:chunk]]
        for step in range(1, NY):
            parts.append(hop(rows[step * chunk : (step + 1) * chunk], dy=-step))
        return jnp.concatenate(parts, axis=0)

    expert_in = to_experts(dot(pick, x_all, ((1,), (0,))).astype(BF16))
    out_grad = to_experts(dot(pick_gate, cot_all, ((1,), (0,))).astype(BF16))

    pre = dot(expert_in, full_in, ((1,), (0,)))
    gate_part, up_part = pre[:, :ff], pre[:, ff:]
    sig_part = jax.nn.sigmoid(gate_part)
    activated = gate_part * sig_part
    hidden = (activated * up_part).astype(BF16)
    expert_out = dot(hidden, full_out, ((1,), (0,))).astype(BF16)
    hidden_grad = dot(out_grad, full_out, ((1,), (1,)))
    slope = sig_part * (1.0 + gate_part * (1.0 - sig_part))
    pre_grad = jnp.concatenate(
        [hidden_grad * up_part * slope, hidden_grad * activated], axis=-1
    ).astype(BF16)
    slot_grad = dot(pre_grad, full_in, ((1,), (1,))).astype(BF16)
    term_in = dot(expert_in, pre_grad, ((0,), (0,))).astype(BF16)
    term_out = dot(hidden, out_grad, ((0,), (0,))).astype(BF16)

    layer_rows = from_experts(expert_out)
    grad_rows = from_experts(slot_grad)
    layer_out = scatter_blocks(dot(pick_gate, layer_rows, ((0,), (0,)))).astype(BF16)
    tokens_grad = scatter_blocks(dot(pick, grad_rows, ((0,), (0,)))).astype(BF16)
    inner = dot(layer_rows, cot_all, ((1,), (1,)))
    inner = jnp.sum(
        jnp.where(place, inner, 0.0).reshape(NY, chunk, width), axis=1
    ).reshape(NY, blocks, 1, tok_rows)
    gate_part_grad = jnp.sum(jnp.where(hits, inner, 0.0), axis=0)
    gate_part_grad = gate_part_grad.reshape(blocks * top_count, tok_rows)
    gate_grad = scatter_blocks(gate_part_grad).T.astype(BF16)

    grad_in = lax.psum_scatter(term_in[None], "dp", scatter_dimension=1, tiled=True).astype(F32)
    grad_out = lax.psum_scatter(term_out[None], "dp", scatter_dimension=1, tiled=True).astype(F32)
    w_in_new, mom_in_new = lion_update(w_in, mom_in, grad_in)
    w_out_new, mom_out_new = lion_update(w_out, mom_out, grad_out)
    return (layer_out, tokens_grad, gate_grad, w_in_new, w_out_new, mom_in_new, mom_out_new)


def solution(mesh):
    token = P(("dp", "expert"), None)
    weight = P("expert", "dp", None)
    in_specs = (token, token, token, token, weight, weight, weight, weight)
    out_specs = (token, token, token, weight, weight, weight, weight)
    return jax.shard_map(body, mesh=mesh, in_specs=in_specs, out_specs=out_specs, check_vma=False)
```

time: 402 us -> 408 us (1.015)
  starting transfers between devices: 30.9 us -> 90.5 us
  waiting for transfers between devices: 271 us -> 219 us
  local copies, waits for them, and re-layouts: 2.36 us -> 13.3 us
  blocking collectives: 10.6 us -> 0 us
  matrix products: 62.9 us -> 52.8 us
  other arithmetic: 8.94 us -> 16.6 us
    all_to_all x5 -> x0, waiting for transfers between devices: 270 us -> none  [the longest x1 92.9 us: body(): lax.all_to_all(from_experts(weighted, groups, local_count, capacity), 'ex...]
    ppermute x0 -> x24, waiting for transfers between devices: none -> 217 us  [hop(): return lax.ppermute(value, 'expert', pairs)]
    ppermute x0 -> x24, starting transfers between devices: none -> 90.3 us  [hop(): return lax.ppermute(value, 'expert', pairs)]
    all_to_all x5 -> x0, starting transfers between devices: 30.5 us -> none  [the longest x1 8.56 us: body(): lax.all_to_all(gate_slots, 'expert', split_axis=0, concat_axis=0, tiled=T...]
    all_to_all x1 -> x0, blocking collectives: 10.6 us -> none  [body(): lax.all_to_all(from_experts(slot_gate, groups, local_count, capacity), 'e...]
    dot_general x12, matrix products: 62.9 us -> 52.8 us  [dot(): return lax.dot_general(a, b, (dims, ((), ())), preferred_element_type=F32)]
    unnamed x13 -> x70, local copies, waits for them, and re-layouts: 0.82 us -> 9.27 us
    convert_element_type x4 -> x7, other arithmetic: 0.63 us -> 5.34 us  [the longest x1 0.95 us: body(): pick_gate = jnp.where(place, gate_wide, 0.0).astype(BF16)]
  transfers between devices with their start and end apart: 9 -> 28, of which waited for: 5 -> 16; matrix products, arithmetic and copies ran while one was open for 14% -> 14% of each run, Pallas kernels for 0% -> 0%
where the time goes in v1:
time: 408 us; the launch traced here: 406 us
  waiting for transfers between devices  219 us (54%)
  starting transfers between devices  90.5 us (22%)
  matrix products  52.8 us (13%)
  other arithmetic  16.6 us (4%)
  between operations  14.3 us (4%)
  local copies, waits for them, and re-layouts  13.3 us (3%)
    ppermute x24, waiting for transfers between devices, hop(): return lax.ppermute(value, 'expert', pairs)  217 us
    ppermute x24, starting transfers between devices, hop(): return lax.ppermute(value, 'expert', pairs)  90.3 us
    dot_general x12, matrix products, dot(): return lax.dot_general(a, b, (dims, ((), ())), preferred_element_type=F32)  52.8 us
    unnamed x70, local copies, waits for them, and re-layouts  9.27 us
  transfers between devices with their start and end apart: 28, of which 16 were waited for; matrix products, arithmetic and copies ran while one was open for 14% of the time, Pallas kernels for 0%

profile of v1, /device:TPU:9, one launch (start us, length us, event | category | flops | bytes accessed | tf_op | source)
XLA Modules:
  0.0 406.1 jit_solution(11253292858655787030)
XLA Ops:
  8.7 3.7 collective-permute-start.2
  13.8 10.4 %collective-permute-done.2 = bf16[128,2048]{1,0:T(8,128)(2,1)S(1)} collective-permute-done((bf16[128,2048]{1,0:T(8,128)(2,1)}, bf16[128,2048]{1,0:T(8,128)(2,1)S(1)}, u32[]{:S(2)}, u32[]{:S(2)}) %collective-permute-start.2) | collective-permute-done | bytes 524320 | tf_op jit(solution)/shard_map/ppermute | solution.py:22
  25.4 59.7 %collective-permute-start.3 = (bf16[256,2048]{1,0:T(8,128)(2,1)S(1)}, bf16[256,2048]{1,0:T(8,128)(2,1)S(1)}, u32[]{:S(2)}, u32[]{:S(2)}) collective-permute-start(bf16[256,2048]{1,0:T(8,128)(2,1)S(1)} %pad_maximum_fusion.6), channel_id=1, source_target_pairs={{0,1},{1,0},{2,3},{3,2},{4,5},{5,4},{6,7},{7,6},{8,9},{9,8},{10,11... | collective-permute-start | bytes 3145736 | tf_op jit(solution)/shard_map/ppermute | solution.py:22
  85.3 2.1 collective-permute-done.1
  91.4 2.3 collective-permute-start.5
  95.3 3.6 collective-permute-start.12
  98.9 40.9 %collective-permute-done.12 = bf16[128,2048]{1,0:T(8,128)(2,1)S(1)} collective-permute-done((bf16[128,2048]{1,0:T(8,128)(2,1)S(1)}, bf16[128,2048]{1,0:T(8,128)(2,1)S(1)}, u32[]{:S(2)}, u32[]{:S(2)}) %collective-permute-start.12) | collective-permute-done | bytes 524320 | tf_op jit(solution)/shard_map/ppermute | solution.py:22
  143.1 9.2 %fusion.3 = f32[768,1536]{1,0:T(8,128)S(1)} fusion(bf16[1,2048,1536]{2,1,0:T(8,128)(2,1)} %all-gather.3.cloned.1.call-done, bf16[192,2048]{1,0:T(8,128)(2,1)} %copy-done.16, bf16[192,2048]{1,0:T(8,128)(2,1)} %copy-done.18, bf16[192,2048]{1,0:T(8,128)(2,1)} %collective-permute-done.4, bf16[192,2048]{1,0:T(8,128)(2,1)S(1)} %get-tuple-element.25), kind=kOutput, calls=%fused_computation.4 | convolution fusion | flops 4844421120 | bytes 14155776 | tf_op jit(solution)/shard_map/dot_general | solution.py:35
  152.4 2.2 copy-done
  155.3 4.7 %convolution_convert_fusion.3 = bf16[768,2048]{1,0:T(8,128)(2,1)S(1)} fusion(bf16[768,768]{1,0:T(8,128)(2,1)S(1)} %multiply_convert_fusion.2, bf16[1,768,2048]{2,1,0:T(8,128)(2,1)} %all-gather.5.cloned.1.call-done), kind=kOutput, calls=%fused_computation.8 | convolution fusion | flops 2417491968 | bytes 7471104 | tf_op jit(solution)/shard_map/dot_general | solution.py:35
  162.5 1.9 collective-permute-start.7
  165.8 13.8 %collective-permute-done.9 = bf16[192,2048]{1,0:T(8,128)(2,1)S(1)} collective-permute-done((bf16[192,2048]{1,0:T(8,128)(2,1)S(1)}, bf16[192,2048]{1,0:T(8,128)(2,1)S(1)}, u32[]{:S(2)}, u32[]{:S(2)}) %collective-permute-start.9) | collective-permute-done | bytes 786464 | tf_op jit(solution)/shard_map/ppermute | solution.py:22
  179.6 2.2 collective-permute-done.8
  181.8 16.6 %collective-permute-done.7 = bf16[192,2048]{1,0:T(8,128)(2,1)S(1)} collective-permute-done((bf16[192,2048]{1,0:T(8,128)(2,1)S(1)}, bf16[192,2048]{1,0:T(8,128)(2,1)S(1)}, u32[]{:S(2)}, u32[]{:S(2)}) %collective-permute-start.7) | collective-permute-done | bytes 786464 | tf_op jit(solution)/shard_map/ppermute | solution.py:22
  204.4 3.4 convolution_convert_fusion.1
  210.3 2.0 collective-permute-start.14
  212.3 14.2 %collective-permute-done.16 = bf16[192,2048]{1,0:T(8,128)(2,1)S(1)} collective-permute-done((bf16[192,2048]{1,0:T(8,128)(2,1)S(1)}, bf16[192,2048]{1,0:T(8,128)(2,1)S(1)}, u32[]{:S(2)}, u32[]{:S(2)}) %collective-permute-start.16) | collective-permute-done | bytes 786464 | tf_op jit(solution)/shard_map/ppermute | solution.py:22
  226.4 17.3 %collective-permute-done.15 = bf16[192,2048]{1,0:T(8,128)(2,1)S(1)} collective-permute-done((bf16[192,2048]{1,0:T(8,128)(2,1)S(1)}, bf16[192,2048]{1,0:T(8,128)(2,1)S(1)}, u32[]{:S(2)}, u32[]{:S(2)}) %collective-permute-start.15) | collective-permute-done | bytes 786464 | tf_op jit(solution)/shard_map/ppermute | solution.py:22
  246.3 4.1 fusion.19
  250.5 7.3 %multiply_convert_fusion.1 = (bf16[768,768]{1,0:T(8,128)(2,1)S(1)}, bf16[768,768]{1,0:T(8,128)(2,1)S(1)}) fusion(f32[768,1536]{1,0:T(8,128)} %copy-done, bf16[1,768,2048]{2,1,0:T(8,128)(2,1)} %all-gather.5.cloned.1.call-done, bf16[192,2048]{1,0:T(8,128)(2,1)} %copy-done.26, bf16[192,2048]{1,0:T(8,128)(2,1)} %copy-done.27, bf16[192,2048]{1,0:T(8,128)(2,1)} %copy-done.28, ...), kind=kOutput, calls=%fused_computation.28 | convolution fusion | flops 2436169728 | bytes 13369344 | tf_op jit(solution)/shard_map/dot_general | solution.py:35
  259.2 8.5 %fusion = bf16[1,2048,1536]{2,1,0:T(8,128)(2,1)} fusion(bf16[768,768]{1,0:T(8,128)(2,1)S(1)} %get-tuple-element.12, bf16[768,768]{1,0:T(8,128)(2,1)S(1)} %get-tuple-element.11, bf16[192,2048]{1,0:T(8,128)(2,1)S(1)} %copy-done.17, bf16[192,2048]{1,0:T(8,128)(2,1)S(1)} %copy-done.19, bf16[192,2048]{1,0:T(8,128)(2,1)} %collective-permute-done.4, ...), kind=kOutput, calls=%fused_computation.1 | convolution fusion | flops 4852285440 | bytes 11796480 | tf_op jit(solution)/shard_map/dot_general | solution.py:35
  269.4 8.2 %fusion.5 = bf16[768,2048]{1,0:T(8,128)(2,1)S(1)} fusion(bf16[1,2048,1536]{2,1,0:T(8,128)(2,1)} %all-gather.3.cloned.1.call-done, bf16[768,768]{1,0:T(8,128)(2,1)S(1)} %copy-done.32, bf16[768,768]{1,0:T(8,128)(2,1)S(1)} %copy-done.30), kind=kOutput, calls=%fused_computation.10 | convolution fusion | flops 4838129664 | bytes 11796480 | tf_op jit(solution)/shard_map/dot_general | solution.py:35
  278.0 2.3 collective-permute-start.19
  280.3 3.1 collective-permute-start.18
  286.8 12.3 %collective-permute-done.19 = bf16[192,2048]{1,0:T(8,128)(2,1)S(1)} collective-permute-done((bf16[192,2048]{1,0:T(8,128)(2,1)S(1)}, bf16[192,2048]{1,0:T(8,128)(2,1)S(1)}, u32[]{:S(2)}, u32[]{:S(2)}) %collective-permute-start.19) | collective-permute-done | bytes 786464 | tf_op jit(solution)/shard_map/ppermute | solution.py:22
  300.5 17.9 %collective-permute-done.17 = bf16[192,2048]{1,0:T(8,128)(2,1)S(1)} collective-permute-done((bf16[192,2048]{1,0:T(8,128)(2,1)S(1)}, bf16[192,2048]{1,0:T(8,128)(2,1)S(1)}, u32[]{:S(2)}, u32[]{:S(2)}) %collective-permute-start.17) | collective-permute-done | bytes 786464 | tf_op jit(solution)/shard_map/ppermute | solution.py:22
  321.0 2.2 collective-permute-done.22
  323.6 3.0 collective-permute-start.11
  328.2 53.4 %collective-permute-done.11 = bf16[128,2048]{1,0:T(8,128)(2,1)S(1)} collective-permute-done((bf16[128,2048]{1,0:T(8,128)(2,1)S(1)}, bf16[128,2048]{1,0:T(8,128)(2,1)S(1)}, u32[]{:S(2)}, u32[]{:S(2)}) %collective-permute-start.11) | collective-permute-done | bytes 524320 | tf_op jit(solution)/shard_map/ppermute | solution.py:22
  382.5 10.3 %collective-permute-done.21 = bf16[128,2048]{1,0:T(8,128)(2,1)S(1)} collective-permute-done((bf16[128,2048]{1,0:T(8,128)(2,1)S(1)}, bf16[128,2048]{1,0:T(8,128)(2,1)S(1)}, u32[]{:S(2)}, u32[]{:S(2)}) %collective-permute-start.21) | collective-permute-done | bytes 524320 | tf_op jit(solution)/shard_map/ppermute | solution.py:22
  393.8 2.4 fusion.39
  396.2 3.4 fusion.30
  (149 shorter events, 43.3 us)
Async XLA Ops:
  7.2 81.8 %copy-start.10 = (bf16[128,2048]{1,0:T(8,128)(2,1)S(1)}, bf16[128,2048]{1,0:T(8,128)(2,1)}, u32[]{:S(2)}) copy-start(bf16[128,2048]{1,0:T(8,128)(2,1)} %param.8) | copy-start | bytes 1572868
  7.2 136.0 %all-gather.3.cloned.1.call-start = ((), (), s32[]{:S(2)}) async-start(), calls=%async_computation.2 | async-start | bytes 7077888 | tf_op jit(solution)/shard_map/all_gather | solution.py:60
  7.9 147.4 %all-gather.5.cloned.1.call-start = ((), (), s32[]{:S(2)}) async-start(), calls=%async_computation.3 | async-start | bytes 3538944 | tf_op jit(solution)/shard_map/all_gather | solution.py:61
  8.7 385.1 %reduce-scatter.5.cloned.1.call-start = ((), (), s32[]{:S(2)}) async-start(), calls=%async_computation.5 | async-start | bytes 3538944 | tf_op jit(solution)/shard_map/reduce_scatter | solution.py:137
  8.7 15.5 %collective-permute-start.2 = (bf16[128,2048]{1,0:T(8,128)(2,1)}, bf16[128,2048]{1,0:T(8,128)(2,1)S(1)}, u32[]{:S(2)}, u32[]{:S(2)}) collective-permute-start(bf16[128,2048]{1,0:T(8,128)(2,1)} %param.8), channel_id=1, source_target_pairs={{0,8},{1,9},{2,10},{3,11},{4,12},{5,13},{6,14},{7,15},{8,0},{9,1},... | collective-permute-start | bytes 1572872 | tf_op jit(solution)/shard_map/ppermute | solution.py:22
  13.8 71.3 %collective-permute-start = (bf16[1,8,128]{2,1,0:T(8,128)(2,1)S(1)}, bf16[1,8,128]{2,1,0:T(8,128)(2,1)S(1)}, u32[]{:S(2)}, u32[]{:S(2)}) collective-permute-start(bf16[1,8,128]{2,1,0:T(8,128)(2,1)S(1)} %maximum_bitcast_fusion), channel_id=1, source_target_pairs={{0,8},{1,9},{2,10},{3,11},{4,12},{5,13},{6,14},{7,15},{8,0},{9,1},... | collective-permute-start | bytes 6152 | tf_op jit(solution)/shard_map/ppermute | solution.py:22
  25.4 63.5 %collective-permute-start.3 = (bf16[256,2048]{1,0:T(8,128)(2,1)S(1)}, bf16[256,2048]{1,0:T(8,128)(2,1)S(1)}, u32[]{:S(2)}, u32[]{:S(2)}) collective-permute-start(bf16[256,2048]{1,0:T(8,128)(2,1)S(1)} %pad_maximum_fusion.6), channel_id=1, source_target_pairs={{0,1},{1,0},{2,3},{3,2},{4,5},{5,4},{6,7},{7,6},{8,9},{9,8},{10,11... | collective-permute-start | bytes 3145736 | tf_op jit(solution)/shard_map/ppermute | solution.py:22
  85.1 2.3 collective-permute-start.1
  91.2 50.2 %collective-permute-start.6 = (bf16[192,2048]{1,0:T(8,128)(2,1)S(1)}, bf16[192,2048]{1,0:T(8,128)(2,1)S(1)}, u32[]{:S(2)}, u32[]{:S(2)}) collective-permute-start(bf16[192,2048]{1,0:T(8,128)(2,1)S(1)} %get-tuple-element.26), channel_id=1, source_target_pairs={{0,6},{1,7},{2,0},{3,1},{4,2},{5,3},{6,4},{7,5},{8,14},{9,15},{10,... | collective-permute-start | bytes 2359304 | tf_op jit(solution)/shard_map/ppermute | solution.py:22
  91.4 50.0 %collective-permute-start.5 = (bf16[192,2048]{1,0:T(8,128)(2,1)S(1)}, bf16[192,2048]{1,0:T(8,128)(2,1)S(1)}, u32[]{:S(2)}, u32[]{:S(2)}) collective-permute-start(bf16[192,2048]{1,0:T(8,128)(2,1)S(1)} %get-tuple-element.27), channel_id=1, source_target_pairs={{0,4},{1,5},{2,6},{3,7},{4,0},{5,1},{6,2},{7,3},{8,12},{9,13},{10,... | collective-permute-start | bytes 2359304 | tf_op jit(solution)/shard_map/ppermute | solution.py:22
  93.7 49.4 %collective-permute-start.4 = (bf16[192,2048]{1,0:T(8,128)(2,1)S(1)}, bf16[192,2048]{1,0:T(8,128)(2,1)}, u32[]{:S(2)}, u32[]{:S(2)}) collective-permute-start(bf16[192,2048]{1,0:T(8,128)(2,1)S(1)} %get-tuple-element.28), channel_id=1, source_target_pairs={{0,2},{1,3},{2,4},{3,5},{4,6},{5,7},{6,0},{7,1},{8,10},{9,11},{10,... | collective-permute-start | bytes 2359304 | tf_op jit(solution)/shard_map/ppermute | solution.py:22
  95.3 44.5 %collective-permute-start.12 = (bf16[128,2048]{1,0:T(8,128)(2,1)S(1)}, bf16[128,2048]{1,0:T(8,128)(2,1)S(1)}, u32[]{:S(2)}, u32[]{:S(2)}) collective-permute-start(bf16[128,2048]{1,0:T(8,128)(2,1)S(1)} %copy-done.2), channel_id=1, source_target_pairs={{0,8},{1,9},{2,10},{3,11},{4,12},{5,13},{6,14},{7,15},{8,0},{9,1},... | collective-permute-start | bytes 1572872 | tf_op jit(solution)/shard_map/ppermute | solution.py:22
  140.9 23.6 %collective-permute-start.13 = (bf16[256,2048]{1,0:T(8,128)(2,1)}, bf16[256,2048]{1,0:T(8,128)(2,1)}, u32[]{:S(2)}, u32[]{:S(2)}) collective-permute-start(bf16[256,2048]{1,0:T(8,128)(2,1)} %pad_maximum_fusion.7), channel_id=1, source_target_pairs={{0,1},{1,0},{2,3},{3,2},{4,5},{5,4},{6,7},{7,6},{8,9},{9,8},{10,11... | collective-permute-start | bytes 3145736 | tf_op jit(solution)/shard_map/ppermute | solution.py:22
  160.4 19.2 %collective-permute-start.9 = (bf16[192,2048]{1,0:T(8,128)(2,1)S(1)}, bf16[192,2048]{1,0:T(8,128)(2,1)S(1)}, u32[]{:S(2)}, u32[]{:S(2)}) collective-permute-start(bf16[192,2048]{1,0:T(8,128)(2,1)S(1)} %get-tuple-element.22), channel_id=1, source_target_pairs={{0,2},{1,3},{2,4},{3,5},{4,6},{5,7},{6,0},{7,1},{8,10},{9,11},{10,... | collective-permute-start | bytes 2359304 | tf_op jit(solution)/shard_map/ppermute | solution.py:22
  161.4 20.4 %collective-permute-start.8 = (bf16[192,2048]{1,0:T(8,128)(2,1)S(1)}, bf16[192,2048]{1,0:T(8,128)(2,1)S(1)}, u32[]{:S(2)}, u32[]{:S(2)}) collective-permute-start(bf16[192,2048]{1,0:T(8,128)(2,1)S(1)} %get-tuple-element.23), channel_id=1, source_target_pairs={{0,4},{1,5},{2,6},{3,7},{4,0},{5,1},{6,2},{7,3},{8,12},{9,13},{10,... | collective-permute-start | bytes 2359304 | tf_op jit(solution)/shard_map/ppermute | solution.py:22
  162.5 35.9 %collective-permute-start.7 = (bf16[192,2048]{1,0:T(8,128)(2,1)S(1)}, bf16[192,2048]{1,0:T(8,128)(2,1)S(1)}, u32[]{:S(2)}, u32[]{:S(2)}) collective-permute-start(bf16[192,2048]{1,0:T(8,128)(2,1)S(1)} %get-tuple-element.24), channel_id=1, source_target_pairs={{0,6},{1,7},{2,0},{3,1},{4,2},{5,3},{6,4},{7,5},{8,14},{9,15},{10,... | collective-permute-start | bytes 2359304 | tf_op jit(solution)/shard_map/ppermute | solution.py:22
  208.2 18.2 %collective-permute-start.16 = (bf16[192,2048]{1,0:T(8,128)(2,1)S(1)}, bf16[192,2048]{1,0:T(8,128)(2,1)S(1)}, u32[]{:S(2)}, u32[]{:S(2)}) collective-permute-start(bf16[192,2048]{1,0:T(8,128)(2,1)S(1)} %get-tuple-element.18), channel_id=1, source_target_pairs={{0,6},{1,7},{2,0},{3,1},{4,2},{5,3},{6,4},{7,5},{8,14},{9,15},{10,... | collective-permute-start | bytes 2359304 | tf_op jit(solution)/shard_map/ppermute | solution.py:22
  208.8 35.0 %collective-permute-start.15 = (bf16[192,2048]{1,0:T(8,128)(2,1)S(1)}, bf16[192,2048]{1,0:T(8,128)(2,1)S(1)}, u32[]{:S(2)}, u32[]{:S(2)}) collective-permute-start(bf16[192,2048]{1,0:T(8,128)(2,1)S(1)} %get-tuple-element.19), channel_id=1, source_target_pairs={{0,4},{1,5},{2,6},{3,7},{4,0},{5,1},{6,2},{7,3},{8,12},{9,13},{10,... | collective-permute-start | bytes 2359304 | tf_op jit(solution)/shard_map/ppermute | solution.py:22
  210.3 35.1 %collective-permute-start.14 = (bf16[192,2048]{1,0:T(8,128)(2,1)S(1)}, bf16[192,2048]{1,0:T(8,128)(2,1)S(1)}, u32[]{:S(2)}, u32[]{:S(2)}) collective-permute-start(bf16[192,2048]{1,0:T(8,128)(2,1)S(1)} %get-tuple-element.20), channel_id=1, source_target_pairs={{0,2},{1,3},{2,4},{3,5},{4,6},{5,7},{6,0},{7,1},{8,10},{9,11},{10,... | collective-permute-start | bytes 2359304 | tf_op jit(solution)/shard_map/ppermute | solution.py:22
  250.4 145.7 %reduce-scatter.3.cloned.1.call-start = ((), (), s32[]{:S(2)}) async-start(), calls=%async_computation.4 | async-start | bytes 7077888 | tf_op jit(solution)/shard_map/reduce_scatter | solution.py:136
  278.0 21.1 %collective-permute-start.19 = (bf16[192,2048]{1,0:T(8,128)(2,1)S(1)}, bf16[192,2048]{1,0:T(8,128)(2,1)S(1)}, u32[]{:S(2)}, u32[]{:S(2)}) collective-permute-start(bf16[192,2048]{1,0:T(8,128)(2,1)S(1)} %get-tuple-element.14), channel_id=1, source_target_pairs={{0,2},{1,3},{2,4},{3,5},{4,6},{5,7},{6,0},{7,1},{8,10},{9,11},{10,... | collective-permute-start | bytes 2359304 | tf_op jit(solution)/shard_map/ppermute | solution.py:22
  280.3 20.2 %collective-permute-start.18 = (bf16[192,2048]{1,0:T(8,128)(2,1)S(1)}, bf16[192,2048]{1,0:T(8,128)(2,1)S(1)}, u32[]{:S(2)}, u32[]{:S(2)}) collective-permute-start(bf16[192,2048]{1,0:T(8,128)(2,1)S(1)} %get-tuple-element.15), channel_id=1, source_target_pairs={{0,4},{1,5},{2,6},{3,7},{4,0},{5,1},{6,2},{7,3},{8,12},{9,13},{10,... | collective-permute-start | bytes 2359304 | tf_op jit(solution)/shard_map/ppermute | solution.py:22
  283.4 35.0 %collective-permute-start.17 = (bf16[192,2048]{1,0:T(8,128)(2,1)S(1)}, bf16[192,2048]{1,0:T(8,128)(2,1)S(1)}, u32[]{:S(2)}, u32[]{:S(2)}) collective-permute-start(bf16[192,2048]{1,0:T(8,128)(2,1)S(1)} %get-tuple-element.16), channel_id=1, source_target_pairs={{0,6},{1,7},{2,0},{3,1},{4,2},{5,3},{6,4},{7,5},{8,14},{9,15},{10,... | collective-permute-start | bytes 2359304 | tf_op jit(solution)/shard_map/ppermute | solution.py:22
  285.4 37.8 %collective-permute-start.10 = (bf16[256,2048]{1,0:T(8,128)(2,1)S(1)}, bf16[256,2048]{1,0:T(8,128)(2,1)S(1)}, u32[]{:S(2)}, u32[]{:S(2)}) collective-permute-start(bf16[256,2048]{1,0:T(8,128)(2,1)S(1)} %slice.196), channel_id=1, source_target_pairs={{0,1},{1,0},{2,3},{3,2},{4,5},{5,4},{6,7},{7,6},{8,9},{9,8},{10,11... | collective-permute-start | bytes 3145736 | tf_op jit(solution)/shard_map/ppermute | solution.py:22
  320.4 6.2 %collective-permute-start.20 = (bf16[256,2048]{1,0:T(8,128)(2,1)S(1)}, bf16[256,2048]{1,0:T(8,128)(2,1)S(1)}, u32[]{:S(2)}, u32[]{:S(2)}) collective-permute-start(bf16[256,2048]{1,0:T(8,128)(2,1)S(1)} %slice.195), channel_id=1, source_target_pairs={{0,1},{1,0},{2,3},{3,2},{4,5},{5,4},{6,7},{7,6},{8,9},{9,8},{10,11... | collective-permute-start | bytes 3145736 | tf_op jit(solution)/shard_map/ppermute | solution.py:22
  320.8 2.3 collective-permute-start.22
  323.1 4.5 %collective-permute-start.23 = (bf16[4,128]{1,0:T(4,128)(2,1)S(1)}, bf16[4,128]{1,0:T(4,128)(2,1)S(1)}, u32[]{:S(2)}, u32[]{:S(2)}) collective-permute-start(bf16[4,128]{1,0:T(4,128)(2,1)S(1)} %slice.138), channel_id=1, source_target_pairs={{0,8},{1,9},{2,10},{3,11},{4,12},{5,13},{6,14},{7,15},{8,0},{9,1},... | collective-permute-start | bytes 3080 | tf_op jit(solution)/shard_map/ppermute | solution.py:22
  323.6 58.0 %collective-permute-start.11 = (bf16[128,2048]{1,0:T(8,128)(2,1)S(1)}, bf16[128,2048]{1,0:T(8,128)(2,1)S(1)}, u32[]{:S(2)}, u32[]{:S(2)}) collective-permute-start(bf16[128,2048]{1,0:T(8,128)(2,1)S(1)} %slice.198), channel_id=1, source_target_pairs={{0,8},{1,9},{2,10},{3,11},{4,12},{5,13},{6,14},{7,15},{8,0},{9,1},... | collective-permute-start | bytes 1572872 | tf_op jit(solution)/shard_map/ppermute | solution.py:22
  326.9 66.9 %copy-start.4 = (bf16[1,96,2048]{2,1,0:T(8,128)(2,1)S(1)}, bf16[1,96,2048]{2,1,0:T(8,128)(2,1)}, u32[]{:S(2)}) copy-start(bf16[1,96,2048]{2,1,0:T(8,128)(2,1)} %param.13) | copy-start | bytes 1179652
  327.0 65.8 %collective-permute-start.21 = (bf16[128,2048]{1,0:T(8,128)(2,1)S(1)}, bf16[128,2048]{1,0:T(8,128)(2,1)S(1)}, u32[]{:S(2)}, u32[]{:S(2)}) collective-permute-start(bf16[128,2048]{1,0:T(8,128)(2,1)S(1)} %slice.197), channel_id=1, source_target_pairs={{0,8},{1,9},{2,10},{3,11},{4,12},{5,13},{6,14},{7,15},{8,0},{9,1},... | collective-permute-start | bytes 1572872 | tf_op jit(solution)/shard_map/ppermute | solution.py:22
  328.2 68.0 %copy-start.1 = (bf16[1,256,1536]{2,1,0:T(8,128)(2,1)S(1)}, bf16[1,256,1536]{2,1,0:T(8,128)(2,1)}, u32[]{:S(2)}) copy-start(bf16[1,256,1536]{2,1,0:T(8,128)(2,1)} %param.12) | copy-start | bytes 2359300
  328.2 68.0 %copy-start.3 = (f32[1,256,1536]{2,1,0:T(8,128)S(1)}, f32[1,256,1536]{2,1,0:T(8,128)}, u32[]{:S(2)}) copy-start(f32[1,256,1536]{2,1,0:T(8,128)} %param.14) | copy-start | bytes 4718596
  (29 other events, 340.8 us)
Sparse Core Ops, SparseCore 0:
  9.7 74.6 all-gather.2
  86.0 40.4 all-gather.4
  250.5 40.6 reduce-scatter.4
  293.5 76.2 reduce-scatter.2
